TPU v7x, 512 devices: a whole 4x4x16 slice. The times are simulated.
512 devices in a mesh: dp: 4 (over x), mp: 128 (over z, y, core).
Axes of the slice: x: 4, y: 4, z: 16, core: 2. Of those that a mesh axis runs over, the one named last changes fastest.
Arguments:
- acts: bfloat16 [8192, 16384], P('dp', 'mp'), may hold values from -6 to 6
- diag_weight: bfloat16 [7, 16384, 128], P(None, 'mp'), may hold values from -0.375 to 0.375
- cross_weight: bfloat16 [7, 16384, 128], P(None, 'mp'), may hold values from -0.375 to 0.375
- low_in: bfloat16 [16384, 64], P('mp'), may hold values from -0.046875 to 0.046875
- low_out: bfloat16 [64, 16384], P(None, 'mp'), may hold values from -0.75 to 0.75
- cotangent: bfloat16 [8192, 16384], P('dp', 'mp'), may hold values from -6 to 6
Outputs:
- output: bfloat16 [8192, 16384], P('dp', 'mp')
- grad_acts: bfloat16 [8192, 16384], P('dp', 'mp')
- grad_diag: float32 [7, 16384, 128], P(None, 'mp')
- grad_cross: float32 [7, 16384, 128], P(None, 'mp')
- grad_low_in: float32 [16384, 64], P('mp')
- grad_low_out: float32 [64, 16384], P(None, 'mp')
All inputs are finite; a program needn't handle non-finite values.
Results may differ from a plain program's by a relative error of at most 0.019.
Values may be sent and summed in bfloat16 or wider, within the bound.
A program may use at most 64 MiB of HBM per device.

v0:
```python
import jax
import jax.numpy as jnp
from jax import lax
from jax.sharding import PartitionSpec as P


def swapped(block, axis, stride):
    count = lax.axis_size(axis)
    route = []
    for low in range(count):
        high = low | 1 << stride
        if high != low and high < count:
            route += [(low, high), (high, low)]
    return lax.ppermute(block, axis, route)


def gelu_slope(pre, cot):
    return jax.vjp(lambda v: jax.nn.gelu(v, approximate=True), pre)[1](cot)[0]


def summed(partial):
    piece = lax.psum_scatter(partial, "mp", scatter_dimension=0, tiled=True)
    return lax.all_gather(piece.astype(jnp.bfloat16), "mp", axis=0, tiled=True)


def rank_total(acts, low_in):
    partial_low = jnp.dot(acts, low_in, preferred_element_type=jnp.float32)
    return summed(partial_low)


def per_device(acts, diag_weight, cross_weight, low_in, low_out, cotangent):
    sections = lax.axis_size("mp").bit_length() - 1
    scale = float(acts.shape[0] * lax.axis_size("dp")) ** (-0.5)
    low = None
    state = acts
    saved = []
    partners = []
    mixed = None
    for section in range(sections):
        other = swapped(state, "mp", section)
        saved.append(state)
        partners.append(other)
        fresh = jnp.dot(state, diag_weight[section], preferred_element_type=jnp.float32)
        fresh = fresh + jnp.dot(other, cross_weight[section], preferred_element_type=jnp.float32)
        if section < sections - 1:
            state = fresh.astype(jnp.bfloat16)
        else:
            mixed = fresh
    low = rank_total(acts, low_in)
    low_b = low.astype(jnp.bfloat16)
    pre = mixed + jnp.dot(low_b, low_out, preferred_element_type=jnp.float32)
    output = jax.nn.gelu(pre, approximate=True).astype(jnp.bfloat16)
    d_pre = gelu_slope(pre, cotangent.astype(jnp.float32)).astype(jnp.bfloat16)
    partial_back = jnp.dot(d_pre, low_out.T, preferred_element_type=jnp.float32)
    d_low = summed(partial_back)
    low_back = jnp.dot(d_low, low_in.T, preferred_element_type=jnp.float32)
    local_in = scale * jnp.dot(acts.T, d_low, preferred_element_type=jnp.float32)
    local_out = scale * jnp.dot(low_b.T, d_pre, preferred_element_type=jnp.float32)
    grad_low_in, grad_low_out = (
        lax.psum(local_in.astype(jnp.bfloat16), "dp").astype(jnp.float32),
        lax.psum(local_out.astype(jnp.bfloat16), "dp").astype(jnp.float32),
    )
    upper = d_pre
    grads_d = [None] * sections
    grads_c = [None] * sections
    grad_acts = None
    for section in range(sections - 1, -1, -1):
        term_d = scale * jnp.dot(saved[section].T, upper, preferred_element_type=jnp.float32)
        term_c = scale * jnp.dot(partners[section].T, upper, preferred_element_type=jnp.float32)
        term_d, term_c = (
            lax.psum(term_d.astype(jnp.bfloat16), "dp").astype(jnp.float32),
            lax.psum(term_c.astype(jnp.bfloat16), "dp").astype(jnp.float32),
        )
        grads_d[section] = term_d
        grads_c[section] = term_c
        sent = jnp.dot(upper, cross_weight[section].T, preferred_element_type=jnp.float32).astype(
            jnp.bfloat16
        )
        arrived = swapped(sent, "mp", section)
        back = jnp.dot(
            upper, diag_weight[section].T, preferred_element_type=jnp.float32
        ) + arrived.astype(jnp.float32)
        if section > 0:
            upper = back.astype(jnp.bfloat16)
        else:
            grad_acts = (back + low_back).astype(jnp.bfloat16)
    grad_diag = jnp.stack(grads_d)
    grad_cross = jnp.stack(grads_c)
    return (output, grad_acts, grad_diag, grad_cross, grad_low_in, grad_low_out)


def solution(mesh):
    placed = (
        P("dp", "mp"),
        P(None, "mp", None),
        P(None, "mp", None),
        P("mp", None),
        P(None, "mp"),
        P("dp", "mp"),
    )
    return jax.shard_map(
        per_device,
        mesh=mesh,
        in_specs=placed,
        out_specs=(
            P("dp", "mp"),
            P("dp", "mp"),
            P(None, "mp", None),
            P(None, "mp", None),
            P("mp", None),
            P(None, "mp"),
        ),
        check_vma=False,
    )
```

profile of v0, /device:TPU:8, one launch (start us, length us, event | category | flops | bytes accessed | tf_op | source)
XLA Modules:
  0.0 965.8 jit_solution(15311273889378741607)
XLA Ops:
  7.2 2.1 collective-permute-start
  9.3 1.3 fusion.90
  12.2 7.7 collective-permute-start.1
  20.2 11.9 %collective-permute-done.1 = bf16[2048,128]{1,0:T(8,128)(2,1)S(1)} collective-permute-done((bf16[2048,128]{1,0:T(8,128)(2,1)S(1)}, bf16[2048,128]{1,0:T(8,128)(2,1)S(1)}, u32[]{:S(2)}, u32[]{:S(2)}) %collective-permute-start.1) | collective-permute-done | bytes 524320 | tf_op jit(solution)/shard_map/ppermute | solution.py:14
  32.9 1.9 collective-permute-start.2
  35.1 14.7 %collective-permute-done.2 = bf16[2048,128]{1,0:T(8,128)(2,1)S(1)} collective-permute-done((bf16[2048,128]{1,0:T(8,128)(2,1)S(1)}, bf16[2048,128]{1,0:T(8,128)(2,1)S(1)}, u32[]{:S(2)}, u32[]{:S(2)}) %collective-permute-start.2) | collective-permute-done | bytes 524320 | tf_op jit(solution)/shard_map/ppermute | solution.py:14
  50.6 1.9 collective-permute-start.3
  52.8 12.2 %collective-permute-done.3 = bf16[2048,128]{1,0:T(8,128)(2,1)S(1)} collective-permute-done((bf16[2048,128]{1,0:T(8,128)(2,1)S(1)}, bf16[2048,128]{1,0:T(8,128)(2,1)S(1)}, u32[]{:S(2)}, u32[]{:S(2)}) %collective-permute-start.3) | collective-permute-done | bytes 524320 | tf_op jit(solution)/shard_map/ppermute | solution.py:14
  65.8 1.9 collective-permute-start.4
  68.0 23.4 %collective-permute-done.4 = bf16[2048,128]{1,0:T(8,128)(2,1)S(1)} collective-permute-done((bf16[2048,128]{1,0:T(8,128)(2,1)S(1)}, bf16[2048,128]{1,0:T(8,128)(2,1)S(1)}, u32[]{:S(2)}, u32[]{:S(2)}) %collective-permute-start.4) | collective-permute-done | bytes 524320 | tf_op jit(solution)/shard_map/ppermute | solution.py:14
  92.2 5.0 collective-permute-start.5
  97.3 1.3 fusion.120
  98.9 44.4 %collective-permute-done.5 = bf16[2048,128]{1,0:T(8,128)(2,1)} collective-permute-done((bf16[2048,128]{1,0:T(8,128)(2,1)S(1)}, bf16[2048,128]{1,0:T(8,128)(2,1)}, u32[]{:S(2)}, u32[]{:S(2)}) %collective-permute-start.5) | collective-permute-done | bytes 524320 | tf_op jit(solution)/shard_map/ppermute | solution.py:14
  143.3 1.3 fusion.6
  144.6 22.4 %collective-permute-start.6 = (bf16[2048,128]{1,0:T(8,128)(2,1)S(1)}, bf16[2048,128]{1,0:T(8,128)(2,1)}, u32[]{:S(2)}, u32[]{:S(2)}) collective-permute-start(bf16[2048,128]{1,0:T(8,128)(2,1)S(1)} %fusion.6), channel_id=1, source_target_pairs={{0,64},{64,0},{1,65},{65,1},{2,66},{66,2},{3,67},{67,3},{4,68},{68... | collective-permute-start | bytes 1572872 | tf_op jit(solution)/shard_map/ppermute | solution.py:14
  167.1 190.0 %reduce-scatter.3.cloned.1.call-done = f32[16,64]{1,0:T(8,128)} async-done(((f32[2048,64]{1,0:T(8,128)}), f32[16,64]{1,0:T(8,128)}) %reduce-scatter.3.cloned.1.call-update) | async-done | bytes 4112 | tf_op jit(solution)/shard_map/reduce_scatter | solution.py:22
  357.8 81.0 %all_gather.6 = bf16[2048,64]{1,0:T(8,128)(2,1)S(1)} all-gather(bf16[16,64]{1,0:T(8,128)(2,1)S(1)} %convert_element_type.179), channel_id=1, replica_groups=mesh['dp'=4,'mp'=128] {'mp'}, dimensions={0}, use_global_device_ids=true | all-gather | bytes 264192 | tf_op jit(solution)/shard_map/all_gather | solution.py:23
  439.1 1.4 convolution_add_fusion.7
  440.5 1.8 fusion.46
  442.6 10.4 %collective-permute-start.7 = (bf16[2048,128]{1,0:T(8,128)(2,1)S(1)}, bf16[2048,128]{1,0:T(8,128)(2,1)S(1)}, u32[]{:S(2)}, u32[]{:S(2)}) collective-permute-start(bf16[2048,128]{1,0:T(8,128)(2,1)S(1)} %convolution_convert_fusion.6), channel_id=1, source_target_pairs={{0,64},{64,0},{1,65},{65,1},{2,66},{66,2},{3,67},{67,3},{4,68},{68... | collective-permute-start | bytes 1572872 | tf_op jit(solution)/shard_map/ppermute | solution.py:14
  453.1 44.2 %collective-permute-done.7 = bf16[2048,128]{1,0:T(8,128)(2,1)S(1)} collective-permute-done((bf16[2048,128]{1,0:T(8,128)(2,1)S(1)}, bf16[2048,128]{1,0:T(8,128)(2,1)S(1)}, u32[]{:S(2)}, u32[]{:S(2)}) %collective-permute-start.7) | collective-permute-done | bytes 524320 | tf_op jit(solution)/shard_map/ppermute | solution.py:14
  497.9 4.7 collective-permute-start.8
  502.6 1.3 fusion.121
  503.9 43.8 %collective-permute-done.8 = bf16[2048,128]{1,0:T(8,128)(2,1)} collective-permute-done((bf16[2048,128]{1,0:T(8,128)(2,1)S(1)}, bf16[2048,128]{1,0:T(8,128)(2,1)}, u32[]{:S(2)}, u32[]{:S(2)}) %collective-permute-start.8) | collective-permute-done | bytes 524320 | tf_op jit(solution)/shard_map/ppermute | solution.py:14
  547.7 1.4 fusion.7
  549.4 1.9 collective-permute-start.9
  552.3 2.0 fusion.27
  555.3 18.4 %collective-permute-done.9 = bf16[2048,128]{1,0:T(8,128)(2,1)S(1)} collective-permute-done((bf16[2048,128]{1,0:T(8,128)(2,1)S(1)}, bf16[2048,128]{1,0:T(8,128)(2,1)S(1)}, u32[]{:S(2)}, u32[]{:S(2)}) %collective-permute-start.9) | collective-permute-done | bytes 524320 | tf_op jit(solution)/shard_map/ppermute | solution.py:14
  573.7 1.1 fusion.8
  574.7 1.1 convolution_convert_fusion.3
  575.8 1.9 collective-permute-start.10
  578.7 2.0 fusion.28
  580.7 183.4 %reduce-scatter.5.cloned.1.call-done = f32[16,64]{1,0:T(8,128)} async-done(((f32[2048,64]{1,0:T(8,128)}), f32[16,64]{1,0:T(8,128)}) %reduce-scatter.5.cloned.1.call-update) | async-done | bytes 4112 | tf_op jit(solution)/shard_map/reduce_scatter | solution.py:22
  764.8 81.2 %all_gather.7 = bf16[2048,64]{1,0:T(8,128)(2,1)S(1)} all-gather(bf16[16,64]{1,0:T(8,128)(2,1)S(1)} %convert_element_type.203), channel_id=1, replica_groups=mesh['dp'=4,'mp'=128] {'mp'}, dimensions={0}, use_global_device_ids=true | all-gather | bytes 264192 | tf_op jit(solution)/shard_map/all_gather | solution.py:23
  846.9 1.4 fusion.9
  848.6 4.1 collective-permute-start.11
  852.7 1.0 fusion.36
  853.7 1.0 fusion.29
  854.7 1.0 fusion.37
  856.8 9.5 collective-permute-done.11
  866.3 1.1 fusion.10
  867.7 3.9 collective-permute-start.12
  875.5 7.7 collective-permute-done.12
  883.2 1.1 fusion.11
  886.8 1.9 collective-permute-start.13
  888.8 55.6 %all-reduce.3.cloned.1.call-done = (bf16[1,128,128]{1,2,0:T(8,128)(2,1)}, bf16[1,128,128]{1,2,0:T(8,128)(2,1)}, bf16[1,128,128]{1,2,0:T(8,128)(2,1)}, bf16[1,128...) async-done(((bf16[1,128,128]{1,2,0:T(8,128)(2,1)}, ...) | async-done | bytes 491536 | tf_op jit(solution)/shard_map/psum | solution.py:71
  944.3 1.3 convert_element_type.223
  957.4 1.9 fusion.12
  (140 shorter events, 32.7 us)
Async XLA Ops:
  7.2 433.3 %copy-start = (bf16[64,128]{1,0:T(8,128)(2,1)S(1)}, bf16[64,128]{1,0:T(8,128)(2,1)}, u32[]{:S(2)}) copy-start(bf16[64,128]{1,0:T(8,128)(2,1)} %param.10) | copy-start | bytes 49156
  7.2 4.2 copy-start.22
  7.2 349.9 %reduce-scatter.3.cloned.1.call-start = ((), (), s32[]{:S(2)}) async-start(), calls=%async_computation.2 | async-start | bytes 1056768 | tf_op jit(solution)/shard_map/reduce_scatter | solution.py:22
  7.2 4.1 collective-permute-start
  10.6 9.3 copy-start.23
  11.4 0.8 copy-start.12
  12.2 19.9 %collective-permute-start.1 = (bf16[2048,128]{1,0:T(8,128)(2,1)S(1)}, bf16[2048,128]{1,0:T(8,128)(2,1)S(1)}, u32[]{:S(2)}, u32[]{:S(2)}) collective-permute-start(bf16[2048,128]{1,0:T(8,128)(2,1)S(1)} %fusion.1), channel_id=1, source_target_pairs={{0,2},{2,0},{1,3},{3,1},{4,6},{6,4},{5,7},{7,5},{8,10},{10,8},{9,1... | collective-permute-start | bytes 1572872 | tf_op jit(solution)/shard_map/ppermute | solution.py:14
  32.1 0.8 copy-start.14
  32.9 16.8 %collective-permute-start.2 = (bf16[2048,128]{1,0:T(8,128)(2,1)S(1)}, bf16[2048,128]{1,0:T(8,128)(2,1)S(1)}, u32[]{:S(2)}, u32[]{:S(2)}) collective-permute-start(bf16[2048,128]{1,0:T(8,128)(2,1)S(1)} %fusion.2), channel_id=1, source_target_pairs={{0,4},{4,0},{1,5},{5,1},{2,6},{6,2},{3,7},{7,3},{8,12},{12,8},{9,1... | collective-permute-start | bytes 1572872 | tf_op jit(solution)/shard_map/ppermute | solution.py:14
  49.8 0.8 copy-start.16
  50.6 2.2 copy-start.2
  50.6 14.4 %collective-permute-start.3 = (bf16[2048,128]{1,0:T(8,128)(2,1)S(1)}, bf16[2048,128]{1,0:T(8,128)(2,1)S(1)}, u32[]{:S(2)}, u32[]{:S(2)}) collective-permute-start(bf16[2048,128]{1,0:T(8,128)(2,1)S(1)} %fusion.3), channel_id=1, source_target_pairs={{0,8},{8,0},{1,9},{9,1},{2,10},{10,2},{3,11},{11,3},{4,12},{12,4},... | collective-permute-start | bytes 1572872 | tf_op jit(solution)/shard_map/ppermute | solution.py:14
  65.0 0.8 copy-start.18
  65.8 2.2 copy-start.4
  65.8 25.6 %collective-permute-start.4 = (bf16[2048,128]{1,0:T(8,128)(2,1)S(1)}, bf16[2048,128]{1,0:T(8,128)(2,1)S(1)}, u32[]{:S(2)}, u32[]{:S(2)}) collective-permute-start(bf16[2048,128]{1,0:T(8,128)(2,1)S(1)} %fusion.4), channel_id=1, source_target_pairs={{0,16},{16,0},{1,17},{17,1},{2,18},{18,2},{3,19},{19,3},{4,20},{20... | collective-permute-start | bytes 1572872 | tf_op jit(solution)/shard_map/ppermute | solution.py:14
  68.0 29.3 %copy-start.1 = (bf16[2048,128]{1,0:T(8,128)(2,1)S(1)}, bf16[2048,128]{1,0:T(8,128)(2,1)}, u32[]{:S(2)}) copy-start(bf16[2048,128]{1,0:T(8,128)(2,1)} %param.6) | copy-start | bytes 1572868
  68.0 29.3 %copy-start.24 = (bf16[128,64]{0,1:T(8,128)(2,1)S(1)}, bf16[128,64]{0,1:T(8,128)(2,1)}, u32[]{:S(2)}) copy-start(bf16[128,64]{0,1:T(8,128)(2,1)} %param.9) | copy-start | bytes 49156
  91.4 0.8 copy-start.20
  92.2 6.4 copy-start.6
  92.2 51.1 %collective-permute-start.5 = (bf16[2048,128]{1,0:T(8,128)(2,1)S(1)}, bf16[2048,128]{1,0:T(8,128)(2,1)}, u32[]{:S(2)}, u32[]{:S(2)}) collective-permute-start(bf16[2048,128]{1,0:T(8,128)(2,1)S(1)} %fusion.5), channel_id=1, source_target_pairs={{0,32},{32,0},{1,33},{33,1},{2,34},{34,2},{3,35},{35,3},{4,36},{36... | collective-permute-start | bytes 1572872 | tf_op jit(solution)/shard_map/ppermute | solution.py:14
  98.6 665.5 %reduce-scatter.5.cloned.1.call-start = ((), (), s32[]{:S(2)}) async-start(), calls=%async_computation.3 | async-start | bytes 1056768 | tf_op jit(solution)/shard_map/reduce_scatter | solution.py:22
  144.6 294.4 %copy-start.8 = (bf16[2048,128]{1,0:T(8,128)(2,1)}, bf16[2048,128]{1,0:T(8,128)(2,1)S(1)}, u32[]{:S(2)}) copy-start(bf16[2048,128]{1,0:T(8,128)(2,1)S(1)} %fusion.6) | copy-start | bytes 1572868
  144.6 294.4 %collective-permute-start.6 = (bf16[2048,128]{1,0:T(8,128)(2,1)S(1)}, bf16[2048,128]{1,0:T(8,128)(2,1)}, u32[]{:S(2)}, u32[]{:S(2)}) collective-permute-start(bf16[2048,128]{1,0:T(8,128)(2,1)S(1)} %fusion.6), channel_id=1, source_target_pairs={{0,64},{64,0},{1,65},{65,1},{2,66},{66,2},{3,67},{67,3},{4,68},{68... | collective-permute-start | bytes 1572872 | tf_op jit(solution)/shard_map/ppermute | solution.py:14
  438.8 1.7 copy-start.10
  439.1 1.4 copy-start.40
  442.6 54.6 %collective-permute-start.7 = (bf16[2048,128]{1,0:T(8,128)(2,1)S(1)}, bf16[2048,128]{1,0:T(8,128)(2,1)S(1)}, u32[]{:S(2)}, u32[]{:S(2)}) collective-permute-start(bf16[2048,128]{1,0:T(8,128)(2,1)S(1)} %convolution_convert_fusion.6), channel_id=1, source_target_pairs={{0,64},{64,0},{1,65},{65,1},{2,66},{66,2},{3,67},{67,3},{4,68},{68... | collective-permute-start | bytes 1572872 | tf_op jit(solution)/shard_map/ppermute | solution.py:14
  497.9 49.9 %collective-permute-start.8 = (bf16[2048,128]{1,0:T(8,128)(2,1)S(1)}, bf16[2048,128]{1,0:T(8,128)(2,1)}, u32[]{:S(2)}, u32[]{:S(2)}) collective-permute-start(bf16[2048,128]{1,0:T(8,128)(2,1)S(1)} %convolution_convert_fusion.5), channel_id=1, source_target_pairs={{0,32},{32,0},{1,33},{33,1},{2,34},{34,2},{3,35},{35,3},{4,36},{36... | collective-permute-start | bytes 1572872 | tf_op jit(solution)/shard_map/ppermute | solution.py:14
  503.9 440.4 %all-reduce.3.cloned.1.call-start = ((), (), s32[]{:S(2)}) async-start(), calls=%async_computation.4 | async-start | bytes 983040 | tf_op jit(solution)/shard_map/psum | solution.py:71
  549.1 2.2 copy-start.9
  549.4 24.2 %collective-permute-start.9 = (bf16[2048,128]{1,0:T(8,128)(2,1)S(1)}, bf16[2048,128]{1,0:T(8,128)(2,1)S(1)}, u32[]{:S(2)}, u32[]{:S(2)}) collective-permute-start(bf16[2048,128]{1,0:T(8,128)(2,1)S(1)} %convolution_convert_fusion.4), channel_id=1, source_target_pairs={{0,16},{16,0},{1,17},{17,1},{2,18},{18,2},{3,19},{19,3},{4,20},{20... | collective-permute-start | bytes 1572872 | tf_op jit(solution)/shard_map/ppermute | solution.py:14
  552.3 2.1 copy-start.11
  574.7 3.0 copy-start.7
  575.8 271.1 %collective-permute-start.10 = (bf16[2048,128]{1,0:T(8,128)(2,1)}, bf16[2048,128]{1,0:T(8,128)(2,1)}, u32[]{:S(2)}, u32[]{:S(2)}) collective-permute-start(bf16[2048,128]{1,0:T(8,128)(2,1)} %convolution_convert_fusion.3), channel_id=1, source_target_pairs={{0,8},{8,0},{1,9},{9,1},{2,10},{10,2},{3,11},{11,3},{4,12},{12,4},... | collective-permute-start | bytes 1572872 | tf_op jit(solution)/shard_map/ppermute | solution.py:14
  848.3 4.5 copy-start.5
  848.6 5.1 copy-start.21
  848.6 17.7 %collective-permute-start.11 = (bf16[2048,128]{1,0:T(8,128)(2,1)S(1)}, bf16[2048,128]{1,0:T(8,128)(2,1)S(1)}, u32[]{:S(2)}, u32[]{:S(2)}) collective-permute-start(bf16[2048,128]{1,0:T(8,128)(2,1)S(1)} %convolution_convert_fusion.2), channel_id=1, source_target_pairs={{0,4},{4,0},{1,5},{5,1},{2,6},{6,2},{3,7},{7,3},{8,12},{12,8},{9,1... | collective-permute-start | bytes 1572872 | tf_op jit(solution)/shard_map/ppermute | solution.py:14
  853.7 1.0 copy-start.3
  854.7 1.0 copy-start.19
  867.7 4.9 copy-start.17
  867.7 15.5 %collective-permute-start.12 = (bf16[2048,128]{1,0:T(8,128)(2,1)S(1)}, bf16[2048,128]{1,0:T(8,128)(2,1)S(1)}, u32[]{:S(2)}, u32[]{:S(2)}) collective-permute-start(bf16[2048,128]{1,0:T(8,128)(2,1)S(1)} %convolution_convert_fusion.1), channel_id=1, source_target_pairs={{0,2},{2,0},{1,3},{3,1},{4,6},{6,4},{5,7},{7,5},{8,10},{10,8},{9,1... | collective-permute-start | bytes 1572872 | tf_op jit(solution)/shard_map/ppermute | solution.py:14
  873.5 1.0 copy-start.15
  884.3 1.0 copy-start.13
  886.8 70.6 %collective-permute-start.13 = (bf16[2048,128]{1,0:T(8,128)(2,1)S(1)}, bf16[2048,128]{1,0:T(8,128)(2,1)S(1)}, u32[]{:S(2)}, u32[]{:S(2)}) collective-permute-start(bf16[2048,128]{1,0:T(8,128)(2,1)S(1)} %convolution_convert_fusion), channel_id=1, source_target_pairs={{0,1},{1,0},{2,3},{3,2},{4,5},{5,4},{6,7},{7,6},{8,9},{9,8},{10,11... | collective-permute-start | bytes 1572872 | tf_op jit(solution)/shard_map/ppermute | solution.py:14
  944.3 1.4 copy-start.39
  946.4 0.8 copy-start.35
  947.2 0.8 copy-start.34
  948.0 0.8 copy-start.33
  954.8 0.8 copy-start.38
  (10 other events, 7.6 us)
Sparse Core Ops, SparseCore 0:
  98.7 258.3 reduce-scatter.2
  504.0 260.0 reduce-scatter.4
  886.4 57.8 all-reduce.2
where the time goes:
time: 968 us; the launch traced here: 966 us
  waiting for transfers between devices  660 us (68%)
  blocking collectives  162 us (17%)
  starting transfers between devices  72 us (7%)
  matrix products  40.1 us (4%)
  between operations  14.3 us (1%)
  local copies, waits for them, and re-layouts  14 us (1%)
    reduce_scatter x2, waiting for transfers between devices, summed(): piece = lax.psum_scatter(partial, 'mp', scatter_dimension=0, tiled=True)  373 us
    ppermute x14, waiting for transfers between devices, swapped(): return lax.ppermute(block, axis, route)  231 us
    all_gather x2, blocking collectives, summed(): return lax.all_gather(piece.astype(jnp.bfloat16), 'mp', axis=0, tiled=True)  162 us
    ppermute x14, starting transfers between devices, swapped(): return lax.ppermute(block, axis, route)  71.9 us
    psum x1, waiting for transfers between devices, per_device(): lax.psum(term_d.astype(jnp.bfloat16), 'dp').astype(jnp.float32)  55.6 us
  transfers between devices with their start and end apart: 17, of which 14 were waited for; matrix products, arithmetic and copies ran while one was open for 3% of the time, Pallas kernels for 0%

commit v1 on v0

--- a/solution.py
+++ b/solution.py
@@ -20,7 +20,10 @@
 
 def summed(partial):
     piece = lax.psum_scatter(partial, "mp", scatter_dimension=0, tiled=True)
-    return lax.all_gather(piece.astype(jnp.bfloat16), "mp", axis=0, tiled=True)
+    return jnp.concatenate(
+        lax.all_to_all(jnp.stack([piece.astype(jnp.bfloat16)] * lax.axis_size("mp")), "mp", 0, 0),
+        axis=0,
+    )
 
 
 def rank_total(acts, low_in):

time: 968 us -> 869 us (0.90)
  blocking collectives: 162 us -> 0 us
  waiting for transfers between devices: 660 us -> 705 us
    all_gather x2 -> x0, blocking collectives: 162 us -> none  [summed(): return lax.all_gather(piece.astype(jnp.bfloat16), 'mp', axis=0, tiled=True)]
    reduce_scatter x2, waiting for transfers between devices: 373 us -> 418 us  [summed(): piece = lax.psum_scatter(partial, 'mp', scatter_dimension=0, tiled=True)]
    all_to_all x0 -> x2, starting transfers between devices: none -> 27.1 us  [summed(): lax.all_to_all(jnp.stack([piece.astype(jnp.bfloat16)] * lax.axis_size('mp...]
    ppermute x14, starting transfers between devices: 71.9 us -> 54 us  [swapped(): return lax.ppermute(block, axis, route)]
    ppermute x14, waiting for transfers between devices: 231 us -> 214 us  [swapped(): return lax.ppermute(block, axis, route)]
    all_to_all x0 -> x2, waiting for transfers between devices: none -> 16.4 us  [summed(): lax.all_to_all(jnp.stack([piece.astype(jnp.bfloat16)] * lax.axis_size('mp...]
  transfers between devices with their start and end apart: 17 -> 19, of which waited for: 14 -> 16; matrix products, arithmetic and copies ran while one was open for 3% -> 5% of each run, Pallas kernels for 0% -> 0%
where the time goes in v1:
time: 869 us; the launch traced here: 866 us
  waiting for transfers between devices  705 us (81%)
  starting transfers between devices  81.2 us (9%)
  matrix products  42.5 us (5%)
  local copies, waits for them, and re-layouts  20.1 us (2%)
  between operations  14.3 us (2%)
    reduce_scatter x2, waiting for transfers between devices, summed(): piece = lax.psum_scatter(partial, 'mp', scatter_dimension=0, tiled=True)  418 us
    ppermute x14, waiting for transfers between devices, swapped(): return lax.ppermute(block, axis, route)  214 us
    psum x1, waiting for transfers between devices, per_device(): lax.psum(term_d.astype(jnp.bfloat16), 'dp').astype(jnp.float32)  56 us
    ppermute x14, starting transfers between devices, swapped(): return lax.ppermute(block, axis, route)  54 us
    all_to_all x2, starting transfers between devices, summed(): lax.all_to_all(jnp.stack([piece.astype(jnp.bfloat16)] * lax.axis_size('mp...  27.1 us
    unnamed x110, local copies, waits for them, and re-layouts  19.1 us
  transfers between devices with their start and end apart: 19, of which 16 were waited for; matrix products, arithmetic and copies ran while one was open for 5% of the time, Pallas kernels for 0%

profile of v1, /device:TPU:8, one launch (start us, length us, event | category | flops | bytes accessed | tf_op | source)
XLA Modules:
  0.0 866.3 jit_solution(6359849745290136738)
XLA Ops:
  7.2 2.1 collective-permute-start
  9.3 1.3 fusion.90
  12.2 7.7 collective-permute-start.1
  20.2 11.9 %collective-permute-done.1 = bf16[2048,128]{1,0:T(8,128)(2,1)S(1)} collective-permute-done((bf16[2048,128]{1,0:T(8,128)(2,1)S(1)}, bf16[2048,128]{1,0:T(8,128)(2,1)S(1)}, u32[]{:S(2)}, u32[]{:S(2)}) %collective-permute-start.1) | collective-permute-done | bytes 524320 | tf_op jit(solution)/shard_map/ppermute | solution.py:14
  32.9 1.9 collective-permute-start.2
  35.1 14.7 %collective-permute-done.2 = bf16[2048,128]{1,0:T(8,128)(2,1)S(1)} collective-permute-done((bf16[2048,128]{1,0:T(8,128)(2,1)S(1)}, bf16[2048,128]{1,0:T(8,128)(2,1)S(1)}, u32[]{:S(2)}, u32[]{:S(2)}) %collective-permute-start.2) | collective-permute-done | bytes 524320 | tf_op jit(solution)/shard_map/ppermute | solution.py:14
  50.6 1.9 collective-permute-start.3
  52.8 12.2 %collective-permute-done.3 = bf16[2048,128]{1,0:T(8,128)(2,1)S(1)} collective-permute-done((bf16[2048,128]{1,0:T(8,128)(2,1)S(1)}, bf16[2048,128]{1,0:T(8,128)(2,1)S(1)}, u32[]{:S(2)}, u32[]{:S(2)}) %collective-permute-start.3) | collective-permute-done | bytes 524320 | tf_op jit(solution)/shard_map/ppermute | solution.py:14
  65.8 1.9 collective-permute-start.4
  67.8 1.3 fusion.120
  69.4 22.1 %collective-permute-done.4 = bf16[2048,128]{1,0:T(8,128)(2,1)S(1)} collective-permute-done((bf16[2048,128]{1,0:T(8,128)(2,1)S(1)}, bf16[2048,128]{1,0:T(8,128)(2,1)S(1)}, u32[]{:S(2)}, u32[]{:S(2)}) %collective-permute-start.4) | collective-permute-done | bytes 524320 | tf_op jit(solution)/shard_map/ppermute | solution.py:14
  92.3 5.0 collective-permute-start.5
  97.3 232.8 %reduce-scatter.3.cloned.1.call-done = f32[16,64]{1,0:T(8,128)} async-done(((f32[2048,64]{1,0:T(8,128)}), f32[16,64]{1,0:T(8,128)}) %reduce-scatter.3.cloned.1.call-update) | async-done | bytes 4112 | tf_op jit(solution)/shard_map/reduce_scatter | solution.py:22
  331.8 13.5 %all-to-all-start = ((bf16[128,2,512]{2,1,0:T(2,128)(2,1)}), bf16[128,2,512]{2,1,0:T(2,128)(2,1)S(1)}, u32[]{:S(2)}, u32[]{:S(2)}) async-start(bf16[128,2,512]{2,1,0:T(2,128)(2,1)} %reshape.24), calls=%async_computation.1 | async-start | bytes 524288 | tf_op jit(solution)/shard_map/all_to_all | solution.py:24
  346.4 1.1 fusion.6
  347.5 12.4 %collective-permute-start.6 = (bf16[2048,128]{1,0:T(8,128)(2,1)S(1)}, bf16[2048,128]{1,0:T(8,128)(2,1)S(1)}, u32[]{:S(2)}, u32[]{:S(2)}) collective-permute-start(bf16[2048,128]{1,0:T(8,128)(2,1)S(1)} %fusion.6), channel_id=1, source_target_pairs={{0,64},{64,0},{1,65},{65,1},{2,66},{66,2},{3,67},{67,3},{4,68},{68... | collective-permute-start | bytes 1572872 | tf_op jit(solution)/shard_map/ppermute | solution.py:14
  360.0 6.6 all-to-all-done
  366.6 1.1 reshape.25
  367.7 1.1 fusion.58
  368.8 43.5 %collective-permute-done.6 = bf16[2048,128]{1,0:T(8,128)(2,1)S(1)} collective-permute-done((bf16[2048,128]{1,0:T(8,128)(2,1)S(1)}, bf16[2048,128]{1,0:T(8,128)(2,1)S(1)}, u32[]{:S(2)}, u32[]{:S(2)}) %collective-permute-start.6) | collective-permute-done | bytes 524320 | tf_op jit(solution)/shard_map/ppermute | solution.py:14
  413.1 1.8 fusion.46
  415.2 6.2 collective-permute-start.7
  421.5 39.5 %collective-permute-done.7 = bf16[2048,128]{1,0:T(8,128)(2,1)S(1)} collective-permute-done((bf16[2048,128]{1,0:T(8,128)(2,1)S(1)}, bf16[2048,128]{1,0:T(8,128)(2,1)S(1)}, u32[]{:S(2)}, u32[]{:S(2)}) %collective-permute-start.7) | collective-permute-done | bytes 524320 | tf_op jit(solution)/shard_map/ppermute | solution.py:14
  462.4 1.9 collective-permute-start.8
  464.3 1.3 fusion.121
  465.6 40.2 %collective-permute-done.8 = bf16[2048,128]{1,0:T(8,128)(2,1)} collective-permute-done((bf16[2048,128]{1,0:T(8,128)(2,1)S(1)}, bf16[2048,128]{1,0:T(8,128)(2,1)}, u32[]{:S(2)}, u32[]{:S(2)}) %collective-permute-start.8) | collective-permute-done | bytes 524320 | tf_op jit(solution)/shard_map/ppermute | solution.py:14
  505.8 1.4 fusion.7
  507.5 2.1 collective-permute-start.9
  512.5 18.8 %collective-permute-done.9 = bf16[2048,128]{1,0:T(8,128)(2,1)S(1)} collective-permute-done((bf16[2048,128]{1,0:T(8,128)(2,1)S(1)}, bf16[2048,128]{1,0:T(8,128)(2,1)S(1)}, u32[]{:S(2)}, u32[]{:S(2)}) %collective-permute-start.9) | collective-permute-done | bytes 524320 | tf_op jit(solution)/shard_map/ppermute | solution.py:14
  531.3 1.1 fusion.8
  532.4 1.1 convolution_convert_fusion.3
  533.5 2.0 collective-permute-start.10
  537.5 185.4 %reduce-scatter.5.cloned.1.call-done = f32[16,64]{1,0:T(8,128)} async-done(((f32[2048,64]{1,0:T(8,128)}), f32[16,64]{1,0:T(8,128)}) %reduce-scatter.5.cloned.1.call-update) | async-done | bytes 4112 | tf_op jit(solution)/shard_map/reduce_scatter | solution.py:22
  724.5 2.1 reshape.26
  726.6 13.6 %all-to-all-start.1 = ((bf16[128,2,512]{2,1,0:T(2,128)(2,1)}), bf16[128,2,512]{2,1,0:T(2,128)(2,1)S(1)}, u32[]{:S(2)}, u32[]{:S(2)}) async-start(bf16[128,2,512]{2,1,0:T(2,128)(2,1)} %reshape.26), calls=%async_computation.3 | async-start | bytes 524288 | tf_op jit(solution)/shard_map/all_to_all | solution.py:24
  742.4 1.4 fusion.9
  743.7 1.9 convolution_convert_fusion.2
  745.6 4.1 collective-permute-start.11
  751.7 9.8 %all-to-all-done.1 = bf16[128,2,512]{2,1,0:T(2,128)(2,1)S(1)} async-done(((bf16[128,2,512]{2,1,0:T(2,128)(2,1)}), bf16[128,2,512]{2,1,0:T(2,128)(2,1)S(1)}, u32[]{:S(2)}, u32[]{:S(2)}) %all-to-all-start.1) | async-done | bytes 262176 | tf_op jit(solution)/shard_map/all_to_all | solution.py:24
  762.8 1.8 collective-permute-done.11
  764.6 1.4 fusion.10
  766.0 1.1 convolution_convert_fusion.1
  767.1 2.8 collective-permute-start.12
  773.9 8.6 collective-permute-done.12
  786.9 1.9 collective-permute-start.13
  788.8 56.0 %all-reduce.3.cloned.1.call-done = (bf16[1,128,128]{1,2,0:T(8,128)(2,1)}, bf16[1,128,128]{1,2,0:T(8,128)(2,1)}, bf16[1,128,128]{1,2,0:T(8,128)(2,1)}, bf16[1,128...) async-done(((bf16[1,128,128]{1,2,0:T(8,128)(2,1)}, ...) | async-done | bytes 491536 | tf_op jit(solution)/shard_map/psum | solution.py:74
  844.8 1.3 convert_element_type.223
  857.9 1.9 fusion.12
  (158 shorter events, 43.3 us)
Async XLA Ops:
  7.2 406.0 %copy-start = (bf16[64,128]{1,0:T(8,128)(2,1)S(1)}, bf16[64,128]{1,0:T(8,128)(2,1)}, u32[]{:S(2)}) copy-start(bf16[64,128]{1,0:T(8,128)(2,1)} %param.10) | copy-start | bytes 49156
  7.2 4.2 copy-start.26
  7.2 322.9 %reduce-scatter.3.cloned.1.call-start = ((), (), s32[]{:S(2)}) async-start(), calls=%async_computation.4 | async-start | bytes 1056768 | tf_op jit(solution)/shard_map/reduce_scatter | solution.py:22
  7.2 4.1 collective-permute-start
  10.6 9.3 %copy-start.28 = (bf16[7,128,128]{2,1,0:T(8,128)(2,1)S(1)}, bf16[7,128,128]{2,1,0:T(8,128)(2,1)}, u32[]{:S(2)}) copy-start(bf16[7,128,128]{2,1,0:T(8,128)(2,1)} %param.7) | copy-start | bytes 688132
  12.2 19.9 %collective-permute-start.1 = (bf16[2048,128]{1,0:T(8,128)(2,1)S(1)}, bf16[2048,128]{1,0:T(8,128)(2,1)S(1)}, u32[]{:S(2)}, u32[]{:S(2)}) collective-permute-start(bf16[2048,128]{1,0:T(8,128)(2,1)S(1)} %fusion.1), channel_id=1, source_target_pairs={{0,2},{2,0},{1,3},{3,1},{4,6},{6,4},{5,7},{7,5},{8,10},{10,8},{9,1... | collective-permute-start | bytes 1572872 | tf_op jit(solution)/shard_map/ppermute | solution.py:14
  32.9 16.8 %collective-permute-start.2 = (bf16[2048,128]{1,0:T(8,128)(2,1)S(1)}, bf16[2048,128]{1,0:T(8,128)(2,1)S(1)}, u32[]{:S(2)}, u32[]{:S(2)}) collective-permute-start(bf16[2048,128]{1,0:T(8,128)(2,1)S(1)} %fusion.2), channel_id=1, source_target_pairs={{0,4},{4,0},{1,5},{5,1},{2,6},{6,2},{3,7},{7,3},{8,12},{12,8},{9,1... | collective-permute-start | bytes 1572872 | tf_op jit(solution)/shard_map/ppermute | solution.py:14
  50.6 2.2 copy-start.2
  50.6 14.4 %collective-permute-start.3 = (bf16[2048,128]{1,0:T(8,128)(2,1)S(1)}, bf16[2048,128]{1,0:T(8,128)(2,1)S(1)}, u32[]{:S(2)}, u32[]{:S(2)}) collective-permute-start(bf16[2048,128]{1,0:T(8,128)(2,1)S(1)} %fusion.3), channel_id=1, source_target_pairs={{0,8},{8,0},{1,9},{9,1},{2,10},{10,2},{3,11},{11,3},{4,12},{12,4},... | collective-permute-start | bytes 1572872 | tf_op jit(solution)/shard_map/ppermute | solution.py:14
  52.8 15.0 %copy-start.1 = (bf16[2048,128]{1,0:T(8,128)(2,1)S(1)}, bf16[2048,128]{1,0:T(8,128)(2,1)}, u32[]{:S(2)}) copy-start(bf16[2048,128]{1,0:T(8,128)(2,1)} %param.6) | copy-start | bytes 1572868
  52.8 15.0 %copy-start.29 = (bf16[128,64]{0,1:T(8,128)(2,1)S(1)}, bf16[128,64]{0,1:T(8,128)(2,1)}, u32[]{:S(2)}) copy-start(bf16[128,64]{0,1:T(8,128)(2,1)} %param.9) | copy-start | bytes 49156
  65.0 0.8 copy-start.18
  65.8 3.2 copy-start.4
  65.8 25.6 %collective-permute-start.4 = (bf16[2048,128]{1,0:T(8,128)(2,1)S(1)}, bf16[2048,128]{1,0:T(8,128)(2,1)S(1)}, u32[]{:S(2)}, u32[]{:S(2)}) collective-permute-start(bf16[2048,128]{1,0:T(8,128)(2,1)S(1)} %fusion.4), channel_id=1, source_target_pairs={{0,16},{16,0},{1,17},{17,1},{2,18},{18,2},{3,19},{19,3},{4,20},{20... | collective-permute-start | bytes 1572872 | tf_op jit(solution)/shard_map/ppermute | solution.py:14
  91.5 0.8 copy-start.20
  92.3 253.1 %copy-start.6 = (bf16[2048,128]{1,0:T(8,128)(2,1)}, bf16[2048,128]{1,0:T(8,128)(2,1)S(1)}, u32[]{:S(2)}) copy-start(bf16[2048,128]{1,0:T(8,128)(2,1)S(1)} %fusion.5) | copy-start | bytes 1572868
  92.3 254.1 %collective-permute-start.5 = (bf16[2048,128]{1,0:T(8,128)(2,1)S(1)}, bf16[2048,128]{1,0:T(8,128)(2,1)S(1)}, u32[]{:S(2)}, u32[]{:S(2)}) collective-permute-start(bf16[2048,128]{1,0:T(8,128)(2,1)S(1)} %fusion.5), channel_id=1, source_target_pairs={{0,32},{32,0},{1,33},{33,1},{2,34},{34,2},{3,35},{35,3},{4,36},{36... | collective-permute-start | bytes 1572872 | tf_op jit(solution)/shard_map/ppermute | solution.py:14
  331.8 34.7 %all-to-all-start = ((bf16[128,2,512]{2,1,0:T(2,128)(2,1)}), bf16[128,2,512]{2,1,0:T(2,128)(2,1)S(1)}, u32[]{:S(2)}, u32[]{:S(2)}) async-start(bf16[128,2,512]{2,1,0:T(2,128)(2,1)} %reshape.24), calls=%async_computation.1 | async-start | bytes 524288 | tf_op jit(solution)/shard_map/all_to_all | solution.py:24
  345.3 377.7 %reduce-scatter.5.cloned.1.call-start = ((), (), s32[]{:S(2)}) async-start(), calls=%async_computation.5 | async-start | bytes 1056768 | tf_op jit(solution)/shard_map/reduce_scatter | solution.py:22
  346.4 1.1 copy-start.22
  347.5 21.3 %copy-start.8 = (bf16[2048,128]{1,0:T(8,128)(2,1)}, bf16[2048,128]{1,0:T(8,128)(2,1)S(1)}, u32[]{:S(2)}) copy-start(bf16[2048,128]{1,0:T(8,128)(2,1)S(1)} %fusion.6) | copy-start | bytes 1572868
  347.5 64.8 %collective-permute-start.6 = (bf16[2048,128]{1,0:T(8,128)(2,1)S(1)}, bf16[2048,128]{1,0:T(8,128)(2,1)S(1)}, u32[]{:S(2)}, u32[]{:S(2)}) collective-permute-start(bf16[2048,128]{1,0:T(8,128)(2,1)S(1)} %fusion.6), channel_id=1, source_target_pairs={{0,64},{64,0},{1,65},{65,1},{2,66},{66,2},{3,67},{67,3},{4,68},{68... | collective-permute-start | bytes 1572872 | tf_op jit(solution)/shard_map/ppermute | solution.py:14
  367.7 44.6 %copy-start.27 = (bf16[7,128,128]{2,1,0:T(8,128)(2,1)S(1)}, bf16[7,128,128]{2,1,0:T(8,128)(2,1)}, u32[]{:S(2)}) copy-start(bf16[7,128,128]{2,1,0:T(8,128)(2,1)} %param.8) | copy-start | bytes 688132
  368.8 44.3 %copy-start.10 = (bf16[128,16,64]{2,1,0:T(8,128)(2,1)S(1)}, bf16[128,16,64]{2,1,0:T(8,128)(2,1)}, u32[]{:S(2)}) copy-start(bf16[128,16,64]{2,1,0:T(8,128)(2,1)} %reshape.25) | copy-start | bytes 786436
  368.8 44.3 %copy-start.45 = (bf16[2048,128]{1,0:T(8,128)(2,1)S(1)}, bf16[2048,128]{1,0:T(8,128)(2,1)}, u32[]{:S(2)}) copy-start(bf16[2048,128]{1,0:T(8,128)(2,1)} %param.11) | copy-start | bytes 1572868
  412.3 0.8 copy-start.24
  415.2 45.8 %collective-permute-start.7 = (bf16[2048,128]{1,0:T(8,128)(2,1)S(1)}, bf16[2048,128]{1,0:T(8,128)(2,1)S(1)}, u32[]{:S(2)}, u32[]{:S(2)}) collective-permute-start(bf16[2048,128]{1,0:T(8,128)(2,1)S(1)} %convolution_convert_fusion.6), channel_id=1, source_target_pairs={{0,64},{64,0},{1,65},{65,1},{2,66},{66,2},{3,67},{67,3},{4,68},{68... | collective-permute-start | bytes 1572872 | tf_op jit(solution)/shard_map/ppermute | solution.py:14
  462.4 43.4 %collective-permute-start.8 = (bf16[2048,128]{1,0:T(8,128)(2,1)S(1)}, bf16[2048,128]{1,0:T(8,128)(2,1)}, u32[]{:S(2)}, u32[]{:S(2)}) collective-permute-start(bf16[2048,128]{1,0:T(8,128)(2,1)S(1)} %convolution_convert_fusion.5), channel_id=1, source_target_pairs={{0,32},{32,0},{1,33},{33,1},{2,34},{34,2},{3,35},{35,3},{4,36},{36... | collective-permute-start | bytes 1572872 | tf_op jit(solution)/shard_map/ppermute | solution.py:14
  507.2 2.4 copy-start.9
  507.5 3.1 copy-start.25
  507.5 23.8 %collective-permute-start.9 = (bf16[2048,128]{1,0:T(8,128)(2,1)S(1)}, bf16[2048,128]{1,0:T(8,128)(2,1)S(1)}, u32[]{:S(2)}, u32[]{:S(2)}) collective-permute-start(bf16[2048,128]{1,0:T(8,128)(2,1)S(1)} %convolution_convert_fusion.4), channel_id=1, source_target_pairs={{0,16},{16,0},{1,17},{17,1},{2,18},{18,2},{3,19},{19,3},{4,20},{20... | collective-permute-start | bytes 1572872 | tf_op jit(solution)/shard_map/ppermute | solution.py:14
  510.5 1.0 copy-start.11
  532.4 3.2 copy-start.7
  533.5 3.0 copy-start.23
  533.5 208.9 %collective-permute-start.10 = (bf16[2048,128]{1,0:T(8,128)(2,1)}, bf16[2048,128]{1,0:T(8,128)(2,1)}, u32[]{:S(2)}, u32[]{:S(2)}) collective-permute-start(bf16[2048,128]{1,0:T(8,128)(2,1)} %convolution_convert_fusion.3), channel_id=1, source_target_pairs={{0,8},{8,0},{1,9},{9,1},{2,10},{10,2},{3,11},{11,3},{4,12},{12,4},... | collective-permute-start | bytes 1572872 | tf_op jit(solution)/shard_map/ppermute | solution.py:14
  724.5 15.8 %copy-start.5 = (bf16[2048,128]{1,0:T(8,128)(2,1)S(1)}, bf16[2048,128]{1,0:T(8,128)(2,1)}, u32[]{:S(2)}) copy-start(bf16[2048,128]{1,0:T(8,128)(2,1)} %copy-done.4) | copy-start | bytes 1572868
  726.6 34.9 %all-to-all-start.1 = ((bf16[128,2,512]{2,1,0:T(2,128)(2,1)}), bf16[128,2,512]{2,1,0:T(2,128)(2,1)S(1)}, u32[]{:S(2)}, u32[]{:S(2)}) async-start(bf16[128,2,512]{2,1,0:T(2,128)(2,1)} %reshape.26), calls=%async_computation.3 | async-start | bytes 524288 | tf_op jit(solution)/shard_map/all_to_all | solution.py:24
  740.3 104.5 %all-reduce.3.cloned.1.call-start = ((), (), s32[]{:S(2)}) async-start(), calls=%async_computation.6 | async-start | bytes 983040 | tf_op jit(solution)/shard_map/psum | solution.py:74
  740.3 1.0 copy-start.21
  743.7 6.0 copy-start.3
  745.6 5.1 copy-start.19
  745.6 19.0 %collective-permute-start.11 = (bf16[2048,128]{1,0:T(8,128)(2,1)}, bf16[2048,128]{1,0:T(8,128)(2,1)}, u32[]{:S(2)}, u32[]{:S(2)}) collective-permute-start(bf16[2048,128]{1,0:T(8,128)(2,1)} %convolution_convert_fusion.2), channel_id=1, source_target_pairs={{0,4},{4,0},{1,5},{5,1},{2,6},{6,2},{3,7},{7,3},{8,12},{12,8},{9,1... | collective-permute-start | bytes 1572872 | tf_op jit(solution)/shard_map/ppermute | solution.py:14
  767.1 3.8 copy-start.17
  767.1 15.4 %collective-permute-start.12 = (bf16[2048,128]{1,0:T(8,128)(2,1)S(1)}, bf16[2048,128]{1,0:T(8,128)(2,1)S(1)}, u32[]{:S(2)}, u32[]{:S(2)}) collective-permute-start(bf16[2048,128]{1,0:T(8,128)(2,1)S(1)} %convolution_convert_fusion.1), channel_id=1, source_target_pairs={{0,2},{2,0},{1,3},{3,1},{4,6},{6,4},{5,7},{7,5},{8,10},{10,8},{9,1... | collective-permute-start | bytes 1572872 | tf_op jit(solution)/shard_map/ppermute | solution.py:14
  771.8 1.0 copy-start.15
  783.5 1.0 copy-start.13
  786.9 71.0 %collective-permute-start.13 = (bf16[2048,128]{1,0:T(8,128)(2,1)S(1)}, bf16[2048,128]{1,0:T(8,128)(2,1)S(1)}, u32[]{:S(2)}, u32[]{:S(2)}) collective-permute-start(bf16[2048,128]{1,0:T(8,128)(2,1)S(1)} %convolution_convert_fusion), channel_id=1, source_target_pairs={{0,1},{1,0},{2,3},{3,2},{4,5},{5,4},{6,7},{7,6},{8,9},{9,8},{10,11... | collective-permute-start | bytes 1572872 | tf_op jit(solution)/shard_map/ppermute | solution.py:14
  844.8 1.4 copy-start.44
  (17 other events, 13.0 us)
Sparse Core Ops, SparseCore 0:
  69.2 260.8 reduce-scatter.2
  465.7 257.1 reduce-scatter.4
  785.7 59.1 all-reduce.2
